TPU v7x, 256 devices: a whole 4x4x8 slice. The times are simulated.
256 devices in a mesh: gx: 32 (over y, x, core), gy: 8 (over z).
Axes of the slice: x: 4, y: 4, z: 8, core: 2. Of those that a mesh axis runs over, the one named last changes fastest.
Arguments:
- displacement: float32 [3, 32, 256, 1024], P(None, None, 'gx', 'gy'), may hold values from -6 to 6
- velocity: float32 [3, 32, 256, 1024], P(None, None, 'gx', 'gy'), may hold values from -6 to 6
- slopes: float32 [2, 32, 256, 1024], P(None, None, 'gx', 'gy'), may hold values from -0.5 to 0.5
- stretch: float32 [32, 256, 1024], P(None, 'gx', 'gy'), may hold values from 0.6 to 1.4
- moduli: float32 [2, 32, 256, 1024], P(None, None, 'gx', 'gy'), may hold values from 0.3 to 1
- buoyancy: float32 [32, 256, 1024], P(None, 'gx', 'gy'), may hold values from 0.5 to 1.5
- probes: float32 [4, 512, 128], P(None, 'gy'), may hold values from -0.0017089844 to 0.0017089844
Outputs:
- final_displacement: float32 [3, 32, 256, 1024], P(None, None, 'gx', 'gy')
- basis: float32 [128, 48, 128], P('gx', 'gy')
- factor: float32 [128, 128], replicated
All inputs are finite; a program needn't handle non-finite values.
Results may differ from a plain program's by a relative error of at most 0.0003.
Values sent between devices are 32-bit elements; how exact they have to be, the bound alone decides.
A program may use at most 64 MiB of HBM per device.

v0:
```python
import math
import jax
import jax.numpy as jnp
from jax import lax
from jax.sharding import PartitionSpec as P

STEPS = 4
time_step = 0.12


def extended(block, sides, width):
    for axis, dim in sides:
        count = lax.axis_size(axis)
        forward = [(i, i + 1) for i in range(count - 1)]
        backward = [(target, source) for source, target in forward]
        low = lax.ppermute(
            lax.slice_in_dim(block, block.shape[dim] - width, None, axis=dim), axis, forward
        )
        high = lax.ppermute(lax.slice_in_dim(block, 0, width, axis=dim), axis, backward)
        block = jnp.concatenate([low, block, high], axis=dim)
    return block


def fourth(values, dimension):
    length_out = values.shape[dimension] - 4

    def segment(offset):
        return lax.slice_in_dim(values, offset, offset + length_out, axis=dimension)

    return (segment(0) - segment(4) + 8.0 * (segment(3) - segment(1))) / 12.0


def vertical(values):
    padded = jnp.pad(values, ((0, 0), (2, 2), (0, 0), (0, 0)))
    return fourth(padded, 1)


def gradient(padded, slope_x, slope_y, stretch):
    d_x = fourth(padded[:, :, :, 2:-2], 2)
    d_y = fourth(padded[:, :, 2:-2, :], 3)
    d_r = vertical(padded[:, :, 2:-2, 2:-2])
    return jnp.stack([d_x + slope_x * d_r, d_y + slope_y * d_r, stretch * d_r], axis=1)


def stresses(gradients, lame, shear):
    divergence = gradients[0, 0] + gradients[1, 1] + gradients[2, 2]
    pressure = lame * divergence
    return jnp.stack(
        [
            pressure + 2.0 * shear * gradients[0, 0],
            pressure + 2.0 * shear * gradients[1, 1],
            pressure + 2.0 * shear * gradients[2, 2],
            shear * (gradients[0, 1] + gradients[1, 0]),
            shear * (gradients[0, 2] + gradients[2, 0]),
            shear * (gradients[1, 2] + gradients[2, 1]),
        ]
    )


def forces(padded, slope_x, slope_y, stretch):
    d_x = fourth(padded[:, :, :, 2:-2], 2)
    d_y = fourth(padded[:, :, 2:-2, :], 3)
    d_r = vertical(padded[:, :, 2:-2, 2:-2])
    rows_x = (0, 3, 4)
    rows_y = (3, 1, 5)
    rows_z = (4, 5, 2)
    return jnp.stack(
        [
            d_x[rows_x[component]]
            + slope_x * d_r[rows_x[component]]
            + d_y[rows_y[component]]
            + slope_y * d_r[rows_y[component]]
            + stretch * d_r[rows_z[component]]
            for component in range(3)
        ]
    )


def lower_factor(gram):
    order = gram.shape[0]
    positions = jnp.arange(order, dtype=jnp.int32)

    def column_step(column_index, lower):
        picker = (positions == column_index).astype(jnp.float32)
        column = jnp.dot(gram, picker, precision=lax.Precision.HIGHEST)
        row_of = jnp.dot(picker, lower, precision=lax.Precision.HIGHEST)
        column = column - jnp.dot(lower, row_of, precision=lax.Precision.HIGHEST)
        pivot = jnp.sqrt(jnp.sum(column * picker))
        entries = jnp.where(
            positions > column_index,
            column / pivot,
            jnp.where(positions == column_index, pivot, 0.0),
        )
        return lower + entries[:, None] * picker[None, :]

    return lax.fori_loop(0, order, column_step, jnp.zeros_like(gram))


def lower_inverse(lower):
    order = lower.shape[0]
    positions = jnp.arange(order, dtype=jnp.int32)

    def row_step(row_index, inverse):
        picker = (positions == row_index).astype(jnp.float32)
        row_of = jnp.dot(picker, lower, precision=lax.Precision.HIGHEST)
        pivot = jnp.sum(row_of * picker)
        fresh = (picker - jnp.dot(row_of, inverse, precision=lax.Precision.HIGHEST)) / pivot
        return inverse + picker[:, None] * fresh[None, :]

    return lax.fori_loop(0, order, row_step, jnp.zeros_like(lower))


def orthogonalize(tall_block, gram):
    lower = lower_factor(gram)
    inverse = lower_inverse(lower)
    result = jnp.dot(
        tall_block, inverse.T, precision=lax.Precision.HIGHEST, preferred_element_type=jnp.float32
    )
    return (result, lower.T)


def shards(displacement, velocity, slopes, stretch, moduli, buoyancy, probes):
    previous = displacement - time_step * velocity
    current = displacement
    for moment in range(STEPS):
        padded = extended(current, (("gx", 2), ("gy", 3)), 2)
        gradients = gradient(padded, slopes[0], slopes[1], stretch)
        stress = extended(stresses(gradients, moduli[0], moduli[1]), (("gx", 2), ("gy", 3)), 2)
        pushes = buoyancy * forces(stress, slopes[0], slopes[1], stretch)
        following = 2.0 * current - previous + time_step**2 * pushes
        velocities = (following - previous) / (2.0 * time_step)
        sampled = velocities[:, ::2, ::2, ::2]
        half_x = sampled.shape[2]
        rearranged = jnp.transpose(sampled, (2, 0, 1, 3)).reshape(-1, sampled.shape[3])
        sketch_term = jnp.dot(
            rearranged,
            probes[moment],
            precision=lax.Precision.HIGHEST,
            preferred_element_type=jnp.float32,
        ).reshape(half_x, -1, probes.shape[2])
        reduced = lax.psum_scatter(sketch_term, "gy", scatter_dimension=1, tiled=True)
        sketch = reduced if moment == 0 else sketch + reduced
        previous, current = (current, following)
    tall_block = sketch.reshape(-1, sketch.shape[2])
    rows_total = tall_block.shape[0] * lax.axis_size("gx") * lax.axis_size("gy")
    gram_local = jnp.dot(
        tall_block.T,
        tall_block,
        precision=lax.Precision.HIGHEST,
        preferred_element_type=jnp.float32,
    )
    gram_whole = lax.psum(gram_local, ("gx", "gy"))
    orthonormal, factor = orthogonalize(tall_block, gram_whole)
    basis = (math.sqrt(rows_total) * orthonormal).reshape(sketch.shape)
    return (current, basis, factor)


def solution(mesh):
    in_specs = (
        P(None, None, "gx", "gy"),
        P(None, None, "gx", "gy"),
        P(None, None, "gx", "gy"),
        P(None, "gx", "gy"),
        P(None, None, "gx", "gy"),
        P(None, "gx", "gy"),
        P(None, "gy", None),
    )
    out_specs = (P(None, None, "gx", "gy"), P("gx", "gy", None), P())
    return jax.shard_map(shards, mesh=mesh, in_specs=in_specs, out_specs=out_specs, check_vma=False)
```

profile of v0, /device:TPU:1, one launch (start us, length us, event | category | flops | bytes accessed | tf_op | source)
XLA Modules:
  0.0 1194.3 jit_solution(5939340690643367252)
XLA Ops:
  8.8 4.6 collective-permute-start
  18.1 4.4 collective-permute-done.1
  26.6 4.9 collective-permute-start.2
  35.1 3.8 fusion.119
  49.6 4.4 collective-permute-done.5
  59.1 3.6 collective-permute-start.6
  76.9 3.5 collective-permute-start.8
  82.4 4.0 collective-permute-done.9
  89.0 3.7 collective-permute-start.10
  107.4 4.4 collective-permute-done.13
  117.2 5.1 collective-permute-start.14
  141.4 6.0 slice.1072
  150.9 3.6 collective-permute-start.18
  163.3 5.1 collective-permute-start.20
  171.9 6.0 slice.1074
  185.3 3.9 collective-permute-start.22
  202.2 5.1 collective-permute-start.24
  225.0 5.1 collective-permute-start.28
  233.0 4.0 collective-permute-done.29
  243.1 3.7 collective-permute-start.30
  266.5 78.0 %all-reduce.14.cloned.1.call-done = f32[4,48,128]{2,0,1:T(4,128)} async-done(((f32[4,48,128]{2,0,1:T(4,128)}), f32[4,48,128]{2,0,1:T(4,128)}) %all-reduce.14.cloned.1.call-update) | async-done | bytes 98320
  347.2 245.3 %all-reduce.12.cloned.1.call-done = f32[128,128]{1,0:T(8,128)} async-done(((f32[128,128]{1,0:T(8,128)}), f32[128,128]{1,0:T(8,128)}) %all-reduce.12.cloned.1.call-update) | async-done | bytes 65552 | tf_op jit(solution)/shard_map/psum | solution.py:152
  592.5 363.3 %while.30 = (s32[]{:T(128)}, f32[128,128]{1,0:T(8,128)S(1)}, f32[128,128]{1,0:T(8,128)}, s32[]{:T(128)}, s32[]{:T(128)}) while((s32[]{:T(128)}, f32[128,128]{1,0:T(8,128)S(1)}, f32[128,128]{1,0:T(8,128)}, s32[]{:T(128)}, s32[]{:T(128)}) %tuple.125), condition=%wide.region_7.8_spmd.clone.clone, body=%wide.region_5.7_spmd.clone.clone.sunk | while | flops 673410 | bytes 332917 | solution.py:96
  956.5 230.0 %while.29 = (s32[]{:T(128)}, f32[128,128]{1,0:T(8,128)S(1)}, f32[128,128]{1,0:T(8,128)S(1)}, s32[]{:T(128)}, s32[]{:T(128)}) while((s32[]{:T(128)}, f32[128,128]{1,0:T(8,128)S(1)}, f32[128,128]{1,0:T(8,128)S(1)}, s32[]{:T(128)}, s32[]{:T(128)}) %tuple.128), condition=%wide.region_10.11_spmd.clone, body=%wide.region_8.10_spmd.clone.sunk | while | flops 460034 | bytes 265316 | solution.py:110
  (1549 shorter events, 667.7 us)
Async XLA Ops:
  7.2 337.4 %all-reduce.14.cloned.1.call-start = ((), (), s32[]{:S(2)}) async-start(), calls=%async_computation.1 | async-start | bytes 196608
  8.8 9.3 collective-permute-start
  13.4 9.1 collective-permute-start.1
  25.3 16.2 %collective-permute-start.3 = (f32[3,32,12,2]{1,3,2,0:T(2,128)}, f32[3,32,12,2]{1,3,2,0:T(2,128)}, u32[]{:S(2)}, u32[]{:S(2)}) collective-permute-start(f32[3,32,12,2]{1,3,2,0:T(2,128)} %get-tuple-element.276), channel_id=1, source_target_pairs={{1,0},{2,1},{3,2},{4,3},{5,4},{6,5},{7,6},{9,8},{10,9},{11,10},{12... | collective-permute-start | bytes 27656 | tf_op jit(solution)/shard_map/ppermute | solution.py:19
  26.6 13.8 %collective-permute-start.2 = (f32[3,32,12,2]{1,3,2,0:T(2,128)}, f32[3,32,12,2]{1,3,2,0:T(2,128)}, u32[]{:S(2)}, u32[]{:S(2)}) collective-permute-start(f32[3,32,12,2]{1,3,2,0:T(2,128)} %get-tuple-element.277), channel_id=1, source_target_pairs={{0,1},{1,2},{2,3},{3,4},{4,5},{5,6},{6,7},{8,9},{9,10},{10,11},{11... | collective-permute-start | bytes 27656 | tf_op jit(solution)/shard_map/ppermute | solution.py:16
  47.0 7.0 collective-permute-start.5
  59.1 10.4 collective-permute-start.6
  80.4 5.9 collective-permute-start.9
  89.0 9.1 collective-permute-start.10
  104.8 7.0 collective-permute-start.13
  117.2 13.2 %collective-permute-start.14 = (f32[6,32,12,2]{1,3,2,0:T(2,128)S(1)}, f32[6,32,12,2]{1,3,2,0:T(2,128)S(1)}, u32[]{:S(2)}, u32[]{:S(2)}) collective-permute-start(f32[6,32,12,2]{1,3,2,0:T(2,128)S(1)} %copy.329), channel_id=1, source_target_pairs={{0,1},{1,2},{2,3},{3,4},{4,5},{5,6},{6,7},{8,9},{9,10},{10,11},{11... | collective-permute-start | bytes 55304 | tf_op jit(solution)/shard_map/ppermute | solution.py:16
  136.6 11.5 collective-permute-start.16
  139.5 8.6 collective-permute-start.17
  150.9 8.8 collective-permute-start.18
  163.3 15.3 %collective-permute-start.20 = (f32[6,32,2,128]{3,1,2,0:T(8,128)S(1)}, f32[6,32,2,128]{3,1,2,0:T(8,128)S(1)}, u32[]{:S(2)}, u32[]{:S(2)}) collective-permute-start(f32[6,32,2,128]{3,1,2,0:T(8,128)S(1)} %get-tuple-element.294), channel_id=1, source_target_pairs={{0,8},{8,16},{16,24},{24,32},{32,40},{40,48},{48,56},{56,64},{64,7... | collective-permute-start | bytes 589832 | tf_op jit(solution)/shard_map/ppermute | solution.py:16
  168.4 10.2 collective-permute-start.21
  185.3 11.0 collective-permute-start.22
  202.2 11.8 collective-permute-start.24
  207.3 6.7 collective-permute-start.25
  214.9 7.5 collective-permute-start.26
  225.0 8.0 collective-permute-start.28
  230.1 7.0 collective-permute-start.29
  243.1 11.6 collective-permute-start.30
  265.2 327.3 %all-reduce.12.cloned.1.call-start = ((), (), s32[]{:S(2)}) async-start(), calls=%async_computation | async-start | bytes 131072 | tf_op jit(solution)/shard_map/psum | solution.py:152
  (52 other events, 254.3 us)
Sparse Core Ops, SparseCore 0:
  265.3 79.1 all-reduce.13
  351.5 240.9 all-reduce.11
where the time goes:
time: 1210 us; the launch traced here: 1190 us
  matrix products  475 us (39%)
  waiting for transfers between devices  362 us (30%)
  loops' own time  98.3 us (8%)
  starting transfers between devices  89 us (7%)
  local copies, waits for them, and re-layouts  85.4 us (7%)
  other arithmetic  68.3 us (6%)
  between operations  15.9 us (1%)
    psum x1, waiting for transfers between devices, shards(): gram_whole = lax.psum(gram_local, ('gx', 'gy'))  245 us
    dot_general x128, matrix products, column_step(): column = jnp.dot(gram, picker, precision=lax.Precision.HIGHEST)  124 us
    dot_general x128, matrix products, column_step(): column = column - jnp.dot(lower, row_of, precision=lax.Precision.HIGHEST)  108 us
    dot_general x128, matrix products, row_step(): jnp.dot(row_of, inverse, precision=lax.Precision.HIGHEST)  107 us
    dot_general x128, matrix products, row_step(): row_of = jnp.dot(picker, lower, precision=lax.Precision.HIGHEST)  105 us
    another operation x1, loops' own time, lower_factor(): return lax.fori_loop(0, order, column_step, jnp.zeros_like(gram))  94 us
    unnamed x3, waiting for transfers between devices  78.1 us
    ppermute x16, starting transfers between devices, extended(): lax.ppermute(lax.slice_in_dim(block, block.shape[dim] - width, None, axis...  62.5 us
  transfers between devices with their start and end apart: 34, of which 17 were waited for; matrix products, arithmetic and copies ran while one was open for 5% of the time, Pallas kernels for 0%

commit v1 on v0

--- a/solution.py
+++ b/solution.py
@@ -6,6 +6,11 @@
 
 STEPS = 4
 time_step = 0.12
+
+
+def by_each_axis(value, inner_axis, outer_axis):
+    partial = lax.psum(value, inner_axis)
+    return lax.psum(partial, outer_axis)
 
 
 def extended(block, sides, width):
@@ -149,7 +154,7 @@
         precision=lax.Precision.HIGHEST,
         preferred_element_type=jnp.float32,
     )
-    gram_whole = lax.psum(gram_local, ("gx", "gy"))
+    gram_whole = by_each_axis(gram_local, "gy", "gx")
     orthonormal, factor = orthogonalize(tall_block, gram_whole)
     basis = (math.sqrt(rows_total) * orthonormal).reshape(sketch.shape)
     return (current, basis, factor)

time: 1210 us -> 1140 us (0.942)
  waiting for transfers between devices: 362 us -> 299 us
    psum x1 -> x2, waiting for transfers between devices: 245 us -> 182 us  [the longest x1 112 us: by_each_axis(): return lax.psum(partial, outer_axis)]
    unnamed x3 -> x4, waiting for transfers between devices: 78.1 us -> 78.1 us
  transfers between devices with their start and end apart: 34 -> 35, of which waited for: 17 -> 18; matrix products, arithmetic and copies ran while one was open for 5% -> 5% of each run, Pallas kernels for 0% -> 0%
where the time goes in v1:
time: 1140 us; the launch traced here: 1130 us
  matrix products  478 us (42%)
  waiting for transfers between devices  299 us (26%)
  loops' own time  97 us (9%)
  starting transfers between devices  89 us (8%)
  local copies, waits for them, and re-layouts  85.4 us (7%)
  other arithmetic  68.3 us (6%)
  between operations  15.6 us (1%)
    dot_general x128, matrix products, column_step(): column = jnp.dot(gram, picker, precision=lax.Precision.HIGHEST)  124 us
    psum x1, waiting for transfers between devices, by_each_axis(): return lax.psum(partial, outer_axis)  112 us
    dot_general x128, matrix products, column_step(): column = column - jnp.dot(lower, row_of, precision=lax.Precision.HIGHEST)  111 us
    dot_general x128, matrix products, row_step(): jnp.dot(row_of, inverse, precision=lax.Precision.HIGHEST)  107 us
    dot_general x128, matrix products, row_step(): row_of = jnp.dot(picker, lower, precision=lax.Precision.HIGHEST)  105 us
    another operation x1, loops' own time, lower_factor(): return lax.fori_loop(0, order, column_step, jnp.zeros_like(gram))  92.8 us
    unnamed x4, waiting for transfers between devices  78.1 us
    psum x1, waiting for transfers between devices, by_each_axis(): partial = lax.psum(value, inner_axis)  70.7 us
  transfers between devices with their start and end apart: 35, of which 18 were waited for; matrix products, arithmetic and copies ran while one was open for 5% of the time, Pallas kernels for 0%

profile of v1, /device:TPU:1, one launch (start us, length us, event | category | flops | bytes accessed | tf_op | source)
XLA Modules:
  0.0 1132.7 jit_solution(15672865155523736554)
XLA Ops:
  8.8 4.6 collective-permute-start
  18.1 4.4 collective-permute-done.1
  26.6 4.9 collective-permute-start.2
  35.1 3.8 fusion.119
  49.6 4.4 collective-permute-done.5
  59.1 3.6 collective-permute-start.6
  82.4 4.0 collective-permute-done.9
  89.0 3.7 collective-permute-start.10
  107.4 4.4 collective-permute-done.13
  117.2 5.1 collective-permute-start.14
  141.4 6.0 slice.1072
  150.9 3.6 collective-permute-start.18
  163.3 5.1 collective-permute-start.20
  171.9 6.0 slice.1074
  185.3 3.9 collective-permute-start.22
  202.2 5.1 collective-permute-start.24
  225.0 5.1 collective-permute-start.28
  233.0 4.0 collective-permute-done.29
  243.1 3.7 collective-permute-start.30
  266.5 78.0 %all-reduce.17.cloned.1.call-done = f32[4,48,128]{2,0,1:T(4,128)} async-done(((f32[4,48,128]{2,0,1:T(4,128)}), f32[4,48,128]{2,0,1:T(4,128)}) %all-reduce.17.cloned.1.call-update) | async-done | bytes 98320
  346.3 70.7 %all-reduce.13.cloned.1.call-done = f32[128,128]{1,0:T(8,128)} async-done(((f32[128,128]{1,0:T(8,128)}), f32[128,128]{1,0:T(8,128)}) %all-reduce.13.cloned.1.call-update) | async-done | bytes 65552 | tf_op jit(solution)/shard_map/psum | solution.py:12
  418.0 111.6 %all-reduce.15.cloned.1.call-done = f32[128,128]{1,0:T(8,128)} async-done(((f32[128,128]{1,0:T(8,128)}), f32[128,128]{1,0:T(8,128)}) %all-reduce.15.cloned.1.call-update) | async-done | bytes 65552 | tf_op jit(solution)/shard_map/psum | solution.py:13
  529.6 365.0 %while.30 = (s32[]{:T(128)}, f32[128,128]{1,0:T(8,128)S(1)}, f32[128,128]{1,0:T(8,128)}, s32[]{:T(128)}, s32[]{:T(128)}) while((s32[]{:T(128)}, f32[128,128]{1,0:T(8,128)S(1)}, f32[128,128]{1,0:T(8,128)}, s32[]{:T(128)}, s32[]{:T(128)}) %tuple.125), condition=%wide.region_8.9_spmd.clone.clone, body=%wide.region_6.8_spmd.clone.clone.sunk | while | flops 673410 | bytes 332917 | solution.py:101
  895.3 230.0 %while.29 = (s32[]{:T(128)}, f32[128,128]{1,0:T(8,128)S(1)}, f32[128,128]{1,0:T(8,128)S(1)}, s32[]{:T(128)}, s32[]{:T(128)}) while((s32[]{:T(128)}, f32[128,128]{1,0:T(8,128)S(1)}, f32[128,128]{1,0:T(8,128)S(1)}, s32[]{:T(128)}, s32[]{:T(128)}) %tuple.128), condition=%wide.region_11.12_spmd.clone, body=%wide.region_9.11_spmd.clone.sunk | while | flops 460034 | bytes 265316 | solution.py:115
  (1552 shorter events, 674.2 us)
Async XLA Ops:
  7.2 337.4 %all-reduce.17.cloned.1.call-start = ((), (), s32[]{:S(2)}) async-start(), calls=%async_computation.2 | async-start | bytes 196608
  8.8 9.3 collective-permute-start
  13.4 9.1 collective-permute-start.1
  25.3 16.2 %collective-permute-start.3 = (f32[3,32,12,2]{1,3,2,0:T(2,128)}, f32[3,32,12,2]{1,3,2,0:T(2,128)}, u32[]{:S(2)}, u32[]{:S(2)}) collective-permute-start(f32[3,32,12,2]{1,3,2,0:T(2,128)} %get-tuple-element.276), channel_id=1, source_target_pairs={{1,0},{2,1},{3,2},{4,3},{5,4},{6,5},{7,6},{9,8},{10,9},{11,10},{12... | collective-permute-start | bytes 27656 | tf_op jit(solution)/shard_map/ppermute | solution.py:24
  26.6 13.8 %collective-permute-start.2 = (f32[3,32,12,2]{1,3,2,0:T(2,128)}, f32[3,32,12,2]{1,3,2,0:T(2,128)}, u32[]{:S(2)}, u32[]{:S(2)}) collective-permute-start(f32[3,32,12,2]{1,3,2,0:T(2,128)} %get-tuple-element.277), channel_id=1, source_target_pairs={{0,1},{1,2},{2,3},{3,4},{4,5},{5,6},{6,7},{8,9},{9,10},{10,11},{11... | collective-permute-start | bytes 27656 | tf_op jit(solution)/shard_map/ppermute | solution.py:21
  47.0 7.0 collective-permute-start.5
  59.1 10.4 collective-permute-start.6
  89.0 9.1 collective-permute-start.10
  104.8 7.0 collective-permute-start.13
  117.2 13.2 %collective-permute-start.14 = (f32[6,32,12,2]{1,3,2,0:T(2,128)S(1)}, f32[6,32,12,2]{1,3,2,0:T(2,128)S(1)}, u32[]{:S(2)}, u32[]{:S(2)}) collective-permute-start(f32[6,32,12,2]{1,3,2,0:T(2,128)S(1)} %copy.329), channel_id=1, source_target_pairs={{0,1},{1,2},{2,3},{3,4},{4,5},{5,6},{6,7},{8,9},{9,10},{10,11},{11... | collective-permute-start | bytes 55304 | tf_op jit(solution)/shard_map/ppermute | solution.py:21
  136.6 11.5 %collective-permute-start.16 = (f32[3,32,2,128]{3,1,2,0:T(8,128)S(1)}, f32[3,32,2,128]{3,1,2,0:T(8,128)S(1)}, u32[]{:S(2)}, u32[]{:S(2)}) collective-permute-start(f32[3,32,2,128]{3,1,2,0:T(8,128)S(1)} %get-tuple-element.316), channel_id=1, source_target_pairs={{0,8},{8,16},{16,24},{24,32},{32,40},{40,48},{48,56},{56,64},{64,7... | collective-permute-start | bytes 294920 | tf_op jit(solution)/shard_map/ppermute | solution.py:21
  139.5 8.6 collective-permute-start.17
  150.9 8.8 collective-permute-start.18
  163.3 15.3 %collective-permute-start.20 = (f32[6,32,2,128]{3,1,2,0:T(8,128)S(1)}, f32[6,32,2,128]{3,1,2,0:T(8,128)S(1)}, u32[]{:S(2)}, u32[]{:S(2)}) collective-permute-start(f32[6,32,2,128]{3,1,2,0:T(8,128)S(1)} %get-tuple-element.294), channel_id=1, source_target_pairs={{0,8},{8,16},{16,24},{24,32},{32,40},{40,48},{48,56},{56,64},{64,7... | collective-permute-start | bytes 589832 | tf_op jit(solution)/shard_map/ppermute | solution.py:21
  168.4 10.2 collective-permute-start.21
  185.3 11.0 collective-permute-start.22
  202.2 11.8 %collective-permute-start.24 = (f32[3,32,2,128]{3,1,2,0:T(8,128)S(1)}, f32[3,32,2,128]{3,1,2,0:T(8,128)S(1)}, u32[]{:S(2)}, u32[]{:S(2)}) collective-permute-start(f32[3,32,2,128]{3,1,2,0:T(8,128)S(1)} %get-tuple-element.312), channel_id=1, source_target_pairs={{0,8},{8,16},{16,24},{24,32},{32,40},{40,48},{48,56},{56,64},{64,7... | collective-permute-start | bytes 294920 | tf_op jit(solution)/shard_map/ppermute | solution.py:21
  207.3 6.7 collective-permute-start.25
  214.9 7.5 collective-permute-start.26
  225.0 8.0 collective-permute-start.28
  230.1 7.0 collective-permute-start.29
  243.1 11.6 %collective-permute-start.30 = (f32[6,32,12,2]{1,3,2,0:T(2,128)S(1)}, f32[6,32,12,2]{1,3,2,0:T(2,128)}, u32[]{:S(2)}, u32[]{:S(2)}) collective-permute-start(f32[6,32,12,2]{1,3,2,0:T(2,128)S(1)} %copy.351), channel_id=1, source_target_pairs={{0,1},{1,2},{2,3},{3,4},{4,5},{5,6},{6,7},{8,9},{9,10},{10,11},{11... | collective-permute-start | bytes 55304 | tf_op jit(solution)/shard_map/ppermute | solution.py:21
  265.2 151.7 %all-reduce.13.cloned.1.call-start = ((), (), s32[]{:S(2)}) async-start(), calls=%async_computation | async-start | bytes 131072 | tf_op jit(solution)/shard_map/psum | solution.py:12
  346.2 183.4 %all-reduce.15.cloned.1.call-start = ((), (), s32[]{:S(2)}) async-start(), calls=%async_computation.1 | async-start | bytes 131072 | tf_op jit(solution)/shard_map/psum | solution.py:13
  (53 other events, 260.2 us)
Sparse Core Ops, SparseCore 0:
  265.3 79.1 all-reduce.16
  347.5 69.3 all-reduce.12
  420.2 109.3 all-reduce.14
